TPU v7x, 32 devices: a whole 2x2x4 slice. The times are simulated.
32 devices in a mesh: fsdp: 2 (over core), expert: 16 (over z, y, x).
Axes of the slice: x: 2, y: 2, z: 4, core: 2. Of those that a mesh axis runs over, the one named last changes fastest.
Arguments:
- tokens: bfloat16 [16, 2048, 1024], P('expert', 'fsdp'), may hold values from -6 to 6
- out_grad: bfloat16 [16, 2048, 1024], P('expert', 'fsdp'), may hold values from -8 to 8
- routes: int32 [16, 2048, 1], P('expert', 'fsdp'), may hold values from 0 to 15; in each aligned block of 1024 rows (0 to 1023, 1024 to 2047, ..., all dimensions but the last counted through in order) at most 128 rows name the same one
- prefix: int32 [16], P('expert'), may hold values from 204 to 1024
- ln1_gain: bfloat16 [1024], P('fsdp'), may hold values from 0.5 to 1.5
- ln1_bias: bfloat16 [1024], P('fsdp'), may hold values from -0.625 to 0.625
- w_qkv: bfloat16 [1024, 3072], P('fsdp'), may hold values from -0.1875 to 0.1875
- q_bias: bfloat16 [1024], P('fsdp'), may hold values from -0.625 to 0.625
- v_bias: bfloat16 [1024], P('fsdp'), may hold values from -0.625 to 0.625
- attention_output_weight: bfloat16 [1024, 1024], P('fsdp'), may hold values from -4 to 4
- attention_output_bias: bfloat16 [1024], P('fsdp'), may hold values from -0.625 to 0.625
- ln2_gain: bfloat16 [1024], P('fsdp'), may hold values from 0.5 to 1.5
- ln2_bias: bfloat16 [1024], P('fsdp'), may hold values from -0.625 to 0.625
- w_router: bfloat16 [1024, 16], P('fsdp'), may hold values from -0.09375 to 0.09375
- moe_bias: bfloat16 [1024], P('fsdp'), may hold values from -0.625 to 0.625
- w_in: bfloat16 [16, 1024, 4096], P('expert', None, 'fsdp'), may hold values from -0.1875 to 0.1875
- w_down: bfloat16 [16, 4096, 1024], P('expert', 'fsdp'), may hold values from -1.5 to 1.5
Outputs:
- out: bfloat16 [16, 2048, 1024], P('expert', 'fsdp')
- d_tokens: bfloat16 [16, 2048, 1024], P('expert', 'fsdp')
- d_ln1_gain: float32 [1024], P(('fsdp', 'expert'))
- d_ln1_bias: float32 [1024], P(('fsdp', 'expert'))
- d_w_qkv: float32 [1024, 3072], P(('fsdp', 'expert'))
- d_q_bias: float32 [1024], P(('fsdp', 'expert'))
- d_v_bias: float32 [1024], P(('fsdp', 'expert'))
- d_w_out: float32 [1024, 1024], P(('fsdp', 'expert'))
- d_out_bias: float32 [1024], P(('fsdp', 'expert'))
- d_ln2_gain: float32 [1024], P(('fsdp', 'expert'))
- d_ln2_bias: float32 [1024], P(('fsdp', 'expert'))
- d_w_router: float32 [1024, 16], P(('fsdp', 'expert'))
- d_moe_bias: float32 [1024], P(('fsdp', 'expert'))
- d_w_in: float32 [16, 1024, 4096], P('expert', None, 'fsdp')
- d_w_down: float32 [16, 4096, 1024], P('expert', 'fsdp')
Inputs may be any that keep to these rules, and one draw needn't show every extreme that they name: `routes`: in each aligned block of 1024 rows (the positions of one sequence on one device) at most 128 rows name the same expert, and some block has 128 that do.
All inputs are finite; a program needn't handle non-finite values.
Results may differ from a plain program's by a relative error of at most 0.02.
Values may be sent and summed in bfloat16 or wider, within the bound.
No kernel may reach another device: no remote copies, remote signals or barrier semaphores. Data moves between devices by JAX's collectives and lax.ppermute only.
A program may use at most 384 MiB of HBM per device.

v0:
```python
from functools import partial
import math
import jax
import jax.numpy as jnp
from jax import lax
from jax.sharding import PartitionSpec as P

HEAD_DIM = 64
NORM_EPSILON = 1e-05
MASK_FILL = -1e30


def passed_along(array, axis, by):
    size = lax.axis_size(axis)
    pairs = [(i, i + by) for i in range(size) if 0 <= i + by < size]
    return lax.ppermute(array, axis, pairs)


def layer_norm(values, norm_gain, norm_bias):
    center = values - jnp.mean(values, axis=-1, keepdims=True)
    inv_std = lax.rsqrt(jnp.mean(center * center, axis=-1, keepdims=True) + NORM_EPSILON)
    normed = center * inv_std
    return (normed * norm_gain + norm_bias, normed, inv_std)


def norm_backward(grad_out, normed, inv_std, norm_gain):
    scaled = grad_out * norm_gain
    return inv_std * (
        scaled
        - jnp.mean(scaled, axis=-1, keepdims=True)
        - normed * jnp.mean(scaled * normed, axis=-1, keepdims=True)
    )


def contract_rows(left_side, right_side):
    return lax.dot_general(
        left_side, right_side, (((0,), (0,)), ((), ())), preferred_element_type=jnp.float32
    )


def contract_last(left_side, right_side):
    return lax.dot_general(
        left_side, right_side, (((1,), (1,)), ((), ())), preferred_element_type=jnp.float32
    )


def visible(query_pos, key_pos, prefix_len):
    keys_row = key_pos[None, :]
    return ((keys_row <= query_pos[:, None]) | (keys_row < prefix_len)) & (keys_row >= 0)


def body(
    tokens,
    out_grad,
    routes,
    prefix,
    ln1_gain,
    ln1_bias,
    w_qkv,
    q_bias,
    v_bias,
    attention_output_weight,
    attention_output_bias,
    ln2_gain,
    ln2_bias,
    w_router,
    moe_bias,
    w_in,
    w_down,
):
    gathered = (
        lax.all_gather(ln1_gain, "fsdp", axis=0, tiled=True),
        lax.all_gather(ln1_bias, "fsdp", axis=0, tiled=True),
        lax.all_gather(w_qkv, "fsdp", axis=0, tiled=True),
        lax.all_gather(q_bias, "fsdp", axis=0, tiled=True),
        lax.all_gather(v_bias, "fsdp", axis=0, tiled=True),
        lax.all_gather(attention_output_weight, "fsdp", axis=0, tiled=True),
        lax.all_gather(attention_output_bias, "fsdp", axis=0, tiled=True),
        lax.all_gather(ln2_gain, "fsdp", axis=0, tiled=True),
        lax.all_gather(ln2_bias, "fsdp", axis=0, tiled=True),
        lax.all_gather(w_router, "fsdp", axis=0, tiled=True),
        lax.all_gather(moe_bias, "fsdp", axis=0, tiled=True),
    )
    qkv_weight = gathered[2]
    out_weight = gathered[5]
    router_weight = gathered[9]
    norm1_gain = gathered[0].astype(jnp.float32)
    norm1_bias = gathered[1].astype(jnp.float32)
    query_bias = gathered[3].astype(jnp.float32)
    value_bias = gathered[4].astype(jnp.float32)
    output_bias = gathered[6].astype(jnp.float32)
    norm2_gain = gathered[7].astype(jnp.float32)
    norm2_bias = gathered[8].astype(jnp.float32)
    expert_bias = gathered[10].astype(jnp.float32)
    row_count = tokens.shape[1]
    model_width = tokens.shape[2]
    head_count = model_width // HEAD_DIM
    query_scale = HEAD_DIM ** (-0.5)
    experts_all = router_weight.shape[1]
    most_slots = max(2, 2 * row_count // experts_all)
    half_index = lax.axis_index("fsdp")
    query_pos = half_index * row_count + jnp.arange(row_count, dtype=jnp.int32)
    key_pos = jnp.concatenate([query_pos - row_count, query_pos])
    prefix_len = prefix[0]
    residual = tokens[0].astype(jnp.float32)
    norm1_out, normed1, inv_std1 = layer_norm(residual, norm1_gain, norm1_bias)
    attn_in = norm1_out.astype(jnp.bfloat16)
    projected = jnp.dot(attn_in, qkv_weight, preferred_element_type=jnp.float32)
    queries = ((projected[:, :model_width] + query_bias) * query_scale).astype(jnp.bfloat16)
    key_value = jnp.concatenate(
        [projected[:, model_width : 2 * model_width], projected[:, 2 * model_width :] + value_bias],
        axis=1,
    ).astype(jnp.bfloat16)
    earlier = passed_along(key_value, "fsdp", 1)
    all_keys = jnp.concatenate([earlier, key_value], axis=0)
    query_heads = queries.reshape(row_count, head_count, HEAD_DIM)
    key_count = all_keys.shape[0]
    block_rows = math.gcd(key_count, 512)

    def key_block(block_index):
        offset = block_index * block_rows
        key_part = lax.dynamic_slice_in_dim(all_keys, offset, block_rows, 0)
        key_heads = key_part[:, :model_width].reshape(block_rows, head_count, HEAD_DIM)
        value_heads = key_part[:, model_width:].reshape(block_rows, head_count, HEAD_DIM)
        allowed = visible(
            query_pos, lax.dynamic_slice_in_dim(key_pos, offset, block_rows, 0), prefix_len
        )[None]
        return (key_heads, value_heads, allowed)

    def forward_block(carried, block_index):
        run_max, run_sum, run_acc = carried
        key_heads, value_heads, allowed = key_block(block_index)
        scores = jnp.einsum(
            "qhd,khd->hqk", query_heads, key_heads, preferred_element_type=jnp.float32
        )
        updated_maximum = jnp.maximum(
            run_max, jnp.max(jnp.where(allowed, scores, MASK_FILL), axis=-1)
        )
        weights = jnp.where(allowed, jnp.exp(scores - updated_maximum[..., None]), 0.0)
        factor = jnp.exp(run_max - updated_maximum)
        run_sum = run_sum * factor + jnp.sum(weights, axis=-1)
        run_acc = run_acc * factor[..., None] + jnp.einsum(
            "hqk,khd->hqd",
            weights.astype(jnp.bfloat16),
            value_heads,
            preferred_element_type=jnp.float32,
        )
        return ((updated_maximum, run_sum, run_acc), None)

    start_state = (
        jnp.full((head_count, row_count), MASK_FILL, jnp.float32),
        jnp.zeros((head_count, row_count), jnp.float32),
        jnp.zeros((head_count, row_count, HEAD_DIM), jnp.float32),
    )
    final_state, unused = lax.scan(forward_block, start_state, jnp.arange(key_count // block_rows))
    run_max, run_sum, run_acc = final_state
    log_sum = run_max + jnp.log(run_sum)
    context_heads = run_acc / run_sum[..., None]
    context_vectors = jnp.transpose(context_heads, (1, 0, 2)).reshape(row_count, model_width)
    context_low = context_vectors.astype(jnp.bfloat16)
    attention_result = (
        jnp.dot(context_low, out_weight, preferred_element_type=jnp.float32) + output_bias
    )
    hidden = residual + attention_result
    norm2_out, normed2, inv_std2 = layer_norm(hidden, norm2_gain, norm2_bias)
    mixed_low = norm2_out.astype(jnp.bfloat16)
    logits = jnp.dot(mixed_low, router_weight, preferred_element_type=jnp.float32)
    router_probs = jax.nn.softmax(logits, axis=-1)
    token_route = routes[0, :, 0]
    one_hot = (token_route[:, None] == jnp.arange(experts_all, dtype=jnp.int32)[None, :]).astype(
        jnp.float32
    )
    gate_value = jnp.sum(router_probs * one_hot, axis=-1)
    earlier_same = jnp.cumsum(one_hot, axis=0) - one_hot
    slot_index = jnp.sum(earlier_same * one_hot, axis=-1).astype(jnp.int32)

    def dispatch(row_values):
        empty_buffer = jnp.zeros((experts_all, most_slots, model_width), row_values.dtype)
        return empty_buffer.at[token_route, slot_index].set(row_values)

    def collect(buffer):
        return buffer[token_route, slot_index]

    arrived = lax.all_to_all(dispatch(mixed_low), "expert", split_axis=0, concat_axis=1, tiled=True)
    owner_in = lax.all_gather(arrived, "fsdp", axis=1, tiled=True)
    pre_act = jnp.einsum("erd,edh->erh", owner_in, w_in, preferred_element_type=jnp.float32)
    activation = jax.nn.gelu(pre_act, approximate=True).astype(jnp.bfloat16)
    partial_out = jnp.einsum("erh,ehd->erd", activation, w_down, preferred_element_type=jnp.float32)
    expert_rows = lax.psum_scatter(
        partial_out.astype(jnp.bfloat16), "fsdp", scatter_dimension=1, tiled=True
    )
    returned = lax.all_to_all(expert_rows, "expert", split_axis=1, concat_axis=0, tiled=True)
    expert_value = collect(returned).astype(jnp.float32)
    output = hidden + gate_value[:, None] * expert_value + expert_bias
    out_cot = out_grad[0].astype(jnp.float32)
    d_expert_bias = jnp.sum(out_cot, axis=0)
    d_gate = jnp.sum(out_cot * expert_value, axis=-1)
    d_expert_value = (gate_value[:, None] * out_cot).astype(jnp.bfloat16)
    grads_arrived = lax.all_to_all(
        dispatch(d_expert_value), "expert", split_axis=0, concat_axis=1, tiled=True
    )
    unused_out, gelu_back = jax.vjp(partial(jax.nn.gelu, approximate=True), pre_act)
    grad_in = lax.all_gather(grads_arrived, "fsdp", axis=1, tiled=True)
    d_activ = jnp.einsum("erd,ehd->erh", grad_in, w_down, preferred_element_type=jnp.float32)
    d_w_down_out = jnp.einsum(
        "erh,erd->ehd", activation, grad_in, preferred_element_type=jnp.float32
    )
    d_pre = gelu_back(d_activ)[0].astype(jnp.bfloat16)
    d_w_in_out = jnp.einsum("erd,erh->edh", owner_in, d_pre, preferred_element_type=jnp.float32)
    d_rows_part = jnp.einsum("erh,edh->erd", d_pre, w_in, preferred_element_type=jnp.float32)
    d_rows = lax.psum_scatter(
        d_rows_part.astype(jnp.bfloat16), "fsdp", scatter_dimension=1, tiled=True
    )
    d_mixed_expert = collect(
        lax.all_to_all(d_rows, "expert", split_axis=1, concat_axis=0, tiled=True)
    ).astype(jnp.float32)
    d_logits = ((d_gate * gate_value)[:, None] * (one_hot - router_probs)).astype(jnp.bfloat16)
    d_mixed = contract_last(d_logits, router_weight) + d_mixed_expert
    d_router = contract_rows(mixed_low, d_logits)
    d_norm2_gain = jnp.sum(d_mixed * normed2, axis=0)
    d_norm2_bias = jnp.sum(d_mixed, axis=0)
    d_hidden = out_cot + norm_backward(d_mixed, normed2, inv_std2, norm2_gain)
    d_attn = d_hidden.astype(jnp.bfloat16)
    d_output_bias = jnp.sum(d_attn.astype(jnp.float32), axis=0)
    d_out_weight = contract_rows(context_low, d_attn)
    d_context = contract_last(d_attn, out_weight).astype(jnp.bfloat16)
    d_context_heads = d_context.reshape(row_count, head_count, HEAD_DIM)
    row_delta = jnp.sum(
        jnp.transpose(d_context_heads.astype(jnp.float32), (1, 0, 2)) * context_heads, axis=-1
    )

    def backward_block(d_query_acc, block_index):
        key_heads, value_heads, allowed = key_block(block_index)
        scores = jnp.einsum(
            "qhd,khd->hqk", query_heads, key_heads, preferred_element_type=jnp.float32
        )
        probs_part = jnp.where(allowed, jnp.exp(scores - log_sum[..., None]), 0.0)
        d_probs = jnp.einsum(
            "qhd,khd->hqk", d_context_heads, value_heads, preferred_element_type=jnp.float32
        )
        d_scores = (probs_part * (d_probs - row_delta[..., None])).astype(jnp.bfloat16)
        d_query_acc = d_query_acc + jnp.einsum(
            "hqk,khd->qhd", d_scores, key_heads, preferred_element_type=jnp.float32
        )
        d_key_part = jnp.einsum(
            "hqk,qhd->khd", d_scores, query_heads, preferred_element_type=jnp.float32
        ).reshape(block_rows, model_width)
        d_value_part = jnp.einsum(
            "hqk,qhd->khd",
            probs_part.astype(jnp.bfloat16),
            d_context_heads,
            preferred_element_type=jnp.float32,
        ).reshape(block_rows, model_width)
        return (d_query_acc, jnp.concatenate([d_key_part, d_value_part], axis=1))

    d_query_sum, d_kv_blocks = lax.scan(
        backward_block,
        jnp.zeros((row_count, head_count, HEAD_DIM), jnp.float32),
        jnp.arange(key_count // block_rows),
    )
    d_kv_all = d_kv_blocks.reshape(key_count, 2 * model_width)
    returned_kv = passed_along(d_kv_all[:row_count].astype(jnp.bfloat16), "fsdp", -1).astype(
        jnp.float32
    )
    d_key_value = (d_kv_all[row_count:] + returned_kv).astype(jnp.bfloat16)
    d_query = (d_query_sum.reshape(row_count, model_width) * query_scale).astype(jnp.bfloat16)
    d_qkv = jnp.concatenate([d_query, d_key_value], axis=1)
    d_query_bias = jnp.sum(d_query.astype(jnp.float32), axis=0)
    d_value_bias = jnp.sum(d_key_value[:, model_width:].astype(jnp.float32), axis=0)
    query_key_value_weight_grad = contract_rows(attn_in, d_qkv)
    d_norm1_out = contract_last(d_qkv, qkv_weight)
    d_norm1_gain = jnp.sum(d_norm1_out * normed1, axis=0)
    d_norm1_bias = jnp.sum(d_norm1_out, axis=0)
    d_tokens = (d_hidden + norm_backward(d_norm1_out, normed1, inv_std1, norm1_gain)).astype(
        jnp.bfloat16
    )
    summed = (
        lax.psum_scatter(d_norm1_gain, ("fsdp", "expert"), scatter_dimension=0, tiled=True),
        lax.psum_scatter(d_norm1_bias, ("fsdp", "expert"), scatter_dimension=0, tiled=True),
        lax.psum_scatter(
            query_key_value_weight_grad, ("fsdp", "expert"), scatter_dimension=0, tiled=True
        ),
        lax.psum_scatter(d_query_bias, ("fsdp", "expert"), scatter_dimension=0, tiled=True),
        lax.psum_scatter(d_value_bias, ("fsdp", "expert"), scatter_dimension=0, tiled=True),
        lax.psum_scatter(d_out_weight, ("fsdp", "expert"), scatter_dimension=0, tiled=True),
        lax.psum_scatter(d_output_bias, ("fsdp", "expert"), scatter_dimension=0, tiled=True),
        lax.psum_scatter(d_norm2_gain, ("fsdp", "expert"), scatter_dimension=0, tiled=True),
        lax.psum_scatter(d_norm2_bias, ("fsdp", "expert"), scatter_dimension=0, tiled=True),
        lax.psum_scatter(d_router, ("fsdp", "expert"), scatter_dimension=0, tiled=True),
        lax.psum_scatter(d_expert_bias, ("fsdp", "expert"), scatter_dimension=0, tiled=True),
    )
    return (
        output.astype(jnp.bfloat16)[None],
        d_tokens[None],
        summed[0],
        summed[1],
        summed[2],
        summed[3],
        summed[4],
        summed[5],
        summed[6],
        summed[7],
        summed[8],
        summed[9],
        summed[10],
        d_w_in_out,
        d_w_down_out,
    )


def solution(mesh):
    return jax.shard_map(
        body,
        mesh=mesh,
        in_specs=(
            P("expert", "fsdp", None),
            P("expert", "fsdp", None),
            P("expert", "fsdp", None),
            P("expert"),
            P("fsdp"),
            P("fsdp"),
            P("fsdp", None),
            P("fsdp"),
            P("fsdp"),
            P("fsdp", None),
            P("fsdp"),
            P("fsdp"),
            P("fsdp"),
            P("fsdp", None),
            P("fsdp"),
            P("expert", None, "fsdp"),
            P("expert", "fsdp", None),
        ),
        out_specs=(
            P("expert", "fsdp", None),
            P("expert", "fsdp", None),
            P(("fsdp", "expert")),
            P(("fsdp", "expert")),
            P(("fsdp", "expert"), None),
            P(("fsdp", "expert")),
            P(("fsdp", "expert")),
            P(("fsdp", "expert"), None),
            P(("fsdp", "expert")),
            P(("fsdp", "expert")),
            P(("fsdp", "expert")),
            P(("fsdp", "expert"), None),
            P(("fsdp", "expert")),
            P("expert", None, "fsdp"),
            P("expert", "fsdp", None),
        ),
        check_vma=False,
    )
```

profile of v0, /device:TPU:0, one launch (start us, length us, event | category | flops | bytes accessed | tf_op | source)
XLA Modules:
  0.0 1677.8 jit_solution(17687012517512811270)
XLA Ops:
  91.9 196.8 %while.28 = (s32[]{:T(128)}, f32[16,1024]{1,0:T(8,128)S(1)}, f32[16,1024]{1,0:T(8,128)S(1)}, f32[16,1024,64]{1,2,0:T(8,128)}, s32[4]{0:T(128)S(1)}, /*index=5*/s...) while((s32[]{:T(128)}, f32[16,1024]{1,0:T(8,128)S(1)}, ...), condition=%wide.region_5.6_spmd.clone, body=%wide.region_2.5_spmd.clone.sunk | while | flops 2219395072 | bytes 120604920 | solution.py:155
  314.3 101.1 %all_to_all.48 = bf16[16,128,1024]{2,1,0:T(8,128)(2,1)} all-to-all(bf16[16,128,1024]{2,1,0:T(8,128)(2,1)} %bitcast.290), channel_id=1, replica_groups=mesh['fsdp'=2,'expert'=16] {'expert'}, dimensions={0} | all-to-all | bytes 8388608 | tf_op jit(solution)/shard_map/all_to_all | solution.py:184
  415.5 18.4 %all-gather.17.cloned.1.call-done = bf16[1,4096,1024]{2,1,0:T(8,128)(2,1)} async-done(((bf16[1,2048,1024]{2,1,0:T(8,128)(2,1)}), bf16[1,4096,1024]{2,1,0:T(8,128)(2,1)}) %all-gather.17.cloned.1.call-update) | async-done | bytes 8388624 | tf_op jit(solution)/shard_map/all_gather | solution.py:185
  433.9 25.7 %fusion.38 = f32[4096,2048]{1,0:T(8,128)} fusion(bf16[1,4096,1024]{2,1,0:T(8,128)(2,1)} %all-gather.17.cloned.1.call-done, bf16[1,1024,2048]{2,1,0:T(8,128)(2,1)} %param.36), kind=kOutput, calls=%fused_computation.63 | convolution fusion | flops 17179869184 | bytes 46137344 | tf_op jit(solution)/shard_map/erd,edh->erh/dot_general | solution.py:186
  459.6 27.6 %convert_bitcast_fusion.1 = bf16[1,4096,1024]{2,1,0:T(8,128)(2,1)} fusion(bf16[1,2048,1024]{2,1,0:T(8,128)(2,1)S(1)} %copy-done.73, f32[4096,2048]{1,0:T(8,128)} %fusion.38), kind=kOutput, calls=%fused_computation.66 | convolution fusion | flops 17259560960 | bytes 46137344 | tf_op jit(solution)/shard_map/erh,ehd->erd/dot_general | solution.py:188
  514.6 26.0 %reduce.9 = bf16[2048,1024]{1,0:T(8,128)(2,1)} reduce(bf16[2048,1,1024]{2,1,0:T(2,128)(2,1)} %bitcast.282, bf16[]{:T(256)} %broadcast.411), dimensions={1}, to_apply=%bitcast.212.reduce_sub_computation | reduce | bytes 8388610
  561.9 77.5 %all-to-all-done.1 = bf16[16,2,65536]{2,1,0:T(2,128)(2,1)} async-done(((bf16[16,2,65536]{2,1,0:T(2,128)(2,1)}), bf16[16,2,65536]{2,1,0:T(2,128)(2,1)}, u32[]{:S(2)}, u32[]{:S(2)}) %all-to-all-start.1) | async-done | bytes 4194336 | tf_op jit(solution)/shard_map/all_to_all | solution.py:192
  658.8 20.9 %gather_fusion = bf16[1024,1024]{1,0:T(8,128)(2,1)} fusion(bf16[16,128,1024]{2,1,0:T(8,128)(2,1)} %bitcast.279, s32[1024]{0:T(1024)S(1)} %bitcast.275), kind=kCustom, calls=%fused_computation | custom fusion | bytes 4202496 | tf_op jit(solution)/shard_map/gather | solution.py:182
  698.6 113.6 %all_to_all.49 = bf16[16,128,1024]{2,1,0:T(8,128)(2,1)} all-to-all(bf16[16,128,1024]{2,1,0:T(8,128)(2,1)} %bitcast.289), channel_id=1, replica_groups=mesh['fsdp'=2,'expert'=16] {'expert'}, dimensions={0} | all-to-all | bytes 8388608 | tf_op jit(solution)/shard_map/all_to_all | solution.py:199
  812.3 18.4 %all-gather.19.cloned.1.call-done = bf16[1,4096,1024]{2,1,0:T(8,128)(2,1)} async-done(((bf16[1,2048,1024]{2,1,0:T(8,128)(2,1)}), bf16[1,4096,1024]{2,1,0:T(8,128)(2,1)}) %all-gather.19.cloned.1.call-update) | async-done | bytes 8388624 | tf_op jit(solution)/shard_map/all_gather | solution.py:203
  830.7 42.2 %fusion.31 = bf16[4096,2048]{1,0:T(8,128)(2,1)} fusion(f32[4096,2048]{1,0:T(8,128)} %fusion.38, bf16[1,4096,1024]{2,1,0:T(8,128)(2,1)} %all-gather.19.cloned.1.call-done, bf16[1,2048,1024]{2,1,0:T(8,128)(2,1)} %param.37), kind=kOutput, calls=%fused_computation.52 | convolution fusion | flops 17347641344 | bytes 62914560 | tf_op jit(solution)/shard_map/erd,ehd->erh/dot_general | solution.py:204
  872.9 23.9 %convert_bitcast_fusion = bf16[1,4096,1024]{2,1,0:T(8,128)(2,1)} fusion(bf16[4096,2048]{1,0:T(8,128)(2,1)} %fusion.31, bf16[1,1024,2048]{2,1,0:T(8,128)(2,1)} %param.36), kind=kOutput, calls=%fused_computation.65 | convolution fusion | flops 17184063488 | bytes 29360128 | tf_op jit(solution)/shard_map/erh,edh->erd/dot_general | solution.py:210
  896.9 18.1 %reduce-scatter.10.cloned.1.call-done = bf16[1,2048,1024]{2,1,0:T(8,128)(2,1)} async-done(((bf16[1,4096,1024]{2,1,0:T(8,128)(2,1)}), bf16[1,2048,1024]{2,1,0:T(8,128)(2,1)}) %reduce-scatter.10.cloned.1.call-update) | async-done | bytes 4194320 | tf_op jit(solution)/shard_map/reduce_scatter | solution.py:211
  923.6 26.0 %reduce.10 = bf16[2048,1024]{1,0:T(8,128)(2,1)} reduce(bf16[2048,1,1024]{2,1,0:T(2,128)(2,1)} %bitcast.283, bf16[]{:T(256)} %broadcast.411), dimensions={1}, to_apply=%bitcast.211.reduce_sub_computation | reduce | bytes 8388610
  971.7 78.2 %all-to-all-done.3 = bf16[16,2,65536]{2,1,0:T(2,128)(2,1)} async-done(((bf16[16,2,65536]{2,1,0:T(2,128)(2,1)}), bf16[16,2,65536]{2,1,0:T(2,128)(2,1)}, u32[]{:S(2)}, u32[]{:S(2)}) %all-to-all-start.3) | async-done | bytes 4194336 | tf_op jit(solution)/shard_map/all_to_all | solution.py:215
  1108.8 351.3 %while.29 = (s32[]{:T(128)}, f32[1024,16,64]{0,2,1:T(8,128)}, f32[4,512,2048]{2,1,0:T(8,128)}, s32[4]{0:T(128)S(1)}, bf16[2048,2048]{0,1:T(8,128)(2,1)}, /*index...) while((s32[]{:T(128)}, f32[1024,16,64]{0,2,1:T(8,128)}, ...), condition=%wide.region_23.24_spmd.clone, body=%wide.region_22.23_spmd.clone.sunk | while | flops 5440538624 | bytes 305875520 | solution.py:256
  1144.4 20.7 %fusion.183 = bf16[16,1024,512]{1,2,0:T(8,128)(2,1)} fusion(f32[16,512,1024]{2,1,0:T(8,128)} %fusion.182, f32[16,1024]{1,0:T(8,128)S(1)} %get-tuple-element.741, f32[16,1024]{1,0:T(8,128)S(1)} %get-tuple-element.739, pred[1024,512]{0,1:T(8,128)(4,1)S(1)} %copy-done.21, bf16[512,16,64]{0,2,1:T(8,128)(2,1)S(1)} %bitcast.286, ...), kind=kOutput, calls=%fused_computation.30.clone.1 | convolution fusion | flops 1115684864 | bytes 54132736 | tf_op jit(solution)/shard_map/while/body/eval_jaxpr/qhd,khd->hqk/dot_general | solution.py:238
  1230.5 20.8 %fusion.183 = bf16[16,1024,512]{1,2,0:T(8,128)(2,1)} fusion(f32[16,512,1024]{2,1,0:T(8,128)} %fusion.182, f32[16,1024]{1,0:T(8,128)S(1)} %get-tuple-element.741, f32[16,1024]{1,0:T(8,128)S(1)} %get-tuple-element.739, pred[1024,512]{0,1:T(8,128)(4,1)S(1)} %copy-done.21, bf16[512,16,64]{0,2,1:T(8,128)(2,1)S(1)} %bitcast.286, ...), kind=kOutput, calls=%fused_computation.30.clone.1 | convolution fusion | flops 1115684864 | bytes 54132736 | tf_op jit(solution)/shard_map/while/body/eval_jaxpr/qhd,khd->hqk/dot_general | solution.py:238
  1318.9 20.7 %fusion.183 = bf16[16,1024,512]{1,2,0:T(8,128)(2,1)} fusion(f32[16,512,1024]{2,1,0:T(8,128)} %fusion.182, f32[16,1024]{1,0:T(8,128)S(1)} %get-tuple-element.741, f32[16,1024]{1,0:T(8,128)S(1)} %get-tuple-element.739, pred[1024,512]{0,1:T(8,128)(4,1)S(1)} %copy-done.21, bf16[512,16,64]{0,2,1:T(8,128)(2,1)S(1)} %bitcast.286, ...), kind=kOutput, calls=%fused_computation.30.clone.1 | convolution fusion | flops 1115684864 | bytes 54132736 | tf_op jit(solution)/shard_map/while/body/eval_jaxpr/qhd,khd->hqk/dot_general | solution.py:238
  1406.9 20.7 %fusion.183 = bf16[16,1024,512]{1,2,0:T(8,128)(2,1)} fusion(f32[16,512,1024]{2,1,0:T(8,128)} %fusion.182, f32[16,1024]{1,0:T(8,128)S(1)} %get-tuple-element.741, f32[16,1024]{1,0:T(8,128)S(1)} %get-tuple-element.739, pred[1024,512]{0,1:T(8,128)(4,1)S(1)} %copy-done.21, bf16[512,16,64]{0,2,1:T(8,128)(2,1)S(1)} %bitcast.286, ...), kind=kOutput, calls=%fused_computation.30.clone.1 | convolution fusion | flops 1115684864 | bytes 54132736 | tf_op jit(solution)/shard_map/while/body/eval_jaxpr/qhd,khd->hqk/dot_general | solution.py:238
  1500.2 24.1 %fusion.51 = f32[1,1024,2048]{2,1,0:T(8,128)} fusion(bf16[4096,2048]{1,0:T(8,128)(2,1)} %fusion.31, bf16[1,4096,1024]{2,1,0:T(8,128)(2,1)} %all-gather.17.cloned.1.call-done), kind=kOutput, calls=%fused_computation.84 | convolution fusion | flops 17179869184 | bytes 33554432 | tf_op jit(solution)/shard_map/erd,erh->edh/dot_general | solution.py:209
  1524.3 26.8 %fusion.54 = f32[1,2048,1024]{2,1,0:T(8,128)} fusion(bf16[1,4096,1024]{2,1,0:T(8,128)(2,1)} %all-gather.19.cloned.1.call-done, f32[4096,2048]{1,0:T(8,128)} %fusion.38), kind=kOutput, calls=%fused_computation.85 | convolution fusion | flops 17255366656 | bytes 50331648 | tf_op jit(solution)/shard_map/erh,erd->ehd/dot_general | solution.py:205
  1578.7 59.0 %all-reduce.8 = (f32[1024]{0:T(1024)S(1)}, f32[1024]{0:T(1024)S(1)}, f32[1024]{0:T(1024)S(1)}, f32[1024]{0:T(1024)S(1)}, f32[1024]{0:T(1024)S(1)}, /*index=5*/f3...) all-reduce(f32[1024]{0:T(1024)S(1)} %get-tuple-element.402, ...), channel_id=4, replica_groups=mesh['fsdp'=2,'expert'=16] {'fsdp','expert'}, use_global_device_ids=true, to_apply=%region_27.28.clone | all-reduce | flops 8192 | bytes 65536
  1652.6 18.4 %reduce-scatter.12.cloned.1.call-done = f32[32,3072]{1,0:T(8,128)} async-done(((f32[1024,3072]{1,0:T(8,128)}), f32[32,3072]{1,0:T(8,128)}) %reduce-scatter.12.cloned.1.call-update) | async-done | bytes 393232 | tf_op jit(solution)/shard_map/reduce_scatter | solution.py:280
  (461 shorter events, 827.3 us)
Async XLA Ops:
  7.2 21.9 %all-gather.13.cloned.1.call-start = ((), (), s32[]{:S(2)}) async-start(), calls=%async_computation.9 | async-start | bytes 9437184 | tf_op jit(solution)/shard_map/all_gather | solution.py:74
  7.9 285.7 %all-gather.15.cloned.1.call-start = ((), (), s32[]{:S(2)}) async-start(), calls=%async_computation.10 | async-start | bytes 3145728 | tf_op jit(solution)/shard_map/all_gather | solution.py:77
  44.1 24.8 %collective-permute-start = (bf16[1024,2048]{1,0:T(8,128)(2,1)}, bf16[1024,2048]{1,0:T(8,128)(2,1)}, u32[]{:S(2)}, u32[]{:S(2)}) collective-permute-start(bf16[1024,2048]{1,0:T(8,128)(2,1)} %pad_maximum_fusion.1), channel_id=1, source_target_pairs={{0,16},{1,17},{2,18},{3,19},{4,20},{5,21},{6,22},{7,23},{8,24},{9,... | collective-permute-start | bytes 12582920 | tf_op jit(solution)/shard_map/ppermute | solution.py:16
  48.2 385.6 %all-gather.17.cloned.1.call-start = ((), (), s32[]{:S(2)}) async-start(), calls=%async_computation.11 | async-start | bytes 12582912 | tf_op jit(solution)/shard_map/all_gather | solution.py:185
  304.8 110.6 %copy-start.40 = (f32[1024]{0:T(1024)}, f32[1024]{0:T(1024)S(1)}, u32[]{:S(2)}) copy-start(f32[1024]{0:T(1024)S(1)} %get-tuple-element.487) | copy-start | bytes 12292
  304.9 110.6 %copy-start.57 = (f32[1024]{0:T(1024)}, f32[1024]{0:T(1024)S(1)}, u32[]{:S(2)}) copy-start(f32[1024]{0:T(1024)S(1)} %fusion.94) | copy-start | bytes 12292
  415.5 89.9 %reduce-scatter.8.cloned.1.call-start = ((), (), s32[]{:S(2)}) async-start(), calls=%async_computation.12 | async-start | bytes 12582912 | tf_op jit(solution)/shard_map/reduce_scatter | solution.py:189
  552.0 87.4 %all-to-all-start.1 = ((bf16[16,2,65536]{2,1,0:T(2,128)(2,1)}), bf16[16,2,65536]{2,1,0:T(2,128)(2,1)}, u32[]{:S(2)}, u32[]{:S(2)}) async-start(bf16[16,2,65536]{2,1,0:T(2,128)(2,1)} %reshape.458), calls=%async_computation.2 | async-start | bytes 8388608 | tf_op jit(solution)/shard_map/all_to_all | solution.py:192
  559.0 271.8 %all-gather.19.cloned.1.call-start = ((), (), s32[]{:S(2)}) async-start(), calls=%async_computation.13 | async-start | bytes 12582912 | tf_op jit(solution)/shard_map/all_gather | solution.py:203
  561.9 121.7 %copy-start.12 = (bf16[1,1024,1024]{1,2,0:T(8,128)(2,1)}, bf16[1,1024,1024]{1,2,0:T(8,128)(2,1)S(1)}, u32[]{:S(2)}) copy-start(bf16[1,1024,1024]{1,2,0:T(8,128)(2,1)S(1)} %copy.135) | copy-start | bytes 6291460
  812.3 102.7 %reduce-scatter.10.cloned.1.call-start = ((), (), s32[]{:S(2)}) async-start(), calls=%async_computation.14 | async-start | bytes 12582912 | tf_op jit(solution)/shard_map/reduce_scatter | solution.py:211
  961.1 88.9 %all-to-all-start.3 = ((bf16[16,2,65536]{2,1,0:T(2,128)(2,1)}), bf16[16,2,65536]{2,1,0:T(2,128)(2,1)}, u32[]{:S(2)}, u32[]{:S(2)}) async-start(bf16[16,2,65536]{2,1,0:T(2,128)(2,1)} %reshape.460), calls=%async_computation.5 | async-start | bytes 8388608 | tf_op jit(solution)/shard_map/all_to_all | solution.py:215
  968.1 530.7 %reduce-scatter.16.cloned.1.call-start = ((), (), s32[]{:S(2)}) async-start(), calls=%async_computation.17 | async-start | bytes 540672
  971.6 681.0 %reduce-scatter.14.cloned.1.call-start = ((), (), s32[]{:S(2)}) async-start(), calls=%async_computation.16 | async-start | bytes 4325376 | tf_op jit(solution)/shard_map/reduce_scatter | solution.py:285
  1107.3 563.7 %reduce-scatter.12.cloned.1.call-start = ((), (), s32[]{:S(2)}) async-start(), calls=%async_computation.15 | async-start | bytes 12976128 | tf_op jit(solution)/shard_map/reduce_scatter | solution.py:280
  1109.0 35.3 %copy-start.36 = (f32[16,1024]{1,0:T(8,128)}, f32[16,1024]{1,0:T(8,128)S(1)}, u32[]{:S(2)}) copy-start(f32[16,1024]{1,0:T(8,128)S(1)} %get-tuple-element.741) | copy-start | bytes 196612 | tf_op jit(solution)/shard_map/while
  1109.0 35.3 %copy-start.45 = (f32[16,1024]{1,0:T(8,128)}, f32[16,1024]{1,0:T(8,128)S(1)}, u32[]{:S(2)}) copy-start(f32[16,1024]{1,0:T(8,128)S(1)} %get-tuple-element.739) | copy-start | bytes 196612 | tf_op jit(solution)/shard_map/while
  1195.0 35.4 %copy-start.36 = (f32[16,1024]{1,0:T(8,128)}, f32[16,1024]{1,0:T(8,128)S(1)}, u32[]{:S(2)}) copy-start(f32[16,1024]{1,0:T(8,128)S(1)} %get-tuple-element.741) | copy-start | bytes 196612 | tf_op jit(solution)/shard_map/while
  1195.0 35.4 %copy-start.45 = (f32[16,1024]{1,0:T(8,128)}, f32[16,1024]{1,0:T(8,128)S(1)}, u32[]{:S(2)}) copy-start(f32[16,1024]{1,0:T(8,128)S(1)} %get-tuple-element.739) | copy-start | bytes 196612 | tf_op jit(solution)/shard_map/while
  1283.5 35.3 %copy-start.36 = (f32[16,1024]{1,0:T(8,128)}, f32[16,1024]{1,0:T(8,128)S(1)}, u32[]{:S(2)}) copy-start(f32[16,1024]{1,0:T(8,128)S(1)} %get-tuple-element.741) | copy-start | bytes 196612 | tf_op jit(solution)/shard_map/while
  1283.5 35.3 %copy-start.45 = (f32[16,1024]{1,0:T(8,128)}, f32[16,1024]{1,0:T(8,128)S(1)}, u32[]{:S(2)}) copy-start(f32[16,1024]{1,0:T(8,128)S(1)} %get-tuple-element.739) | copy-start | bytes 196612 | tf_op jit(solution)/shard_map/while
  1371.7 35.2 %copy-start.36 = (f32[16,1024]{1,0:T(8,128)}, f32[16,1024]{1,0:T(8,128)S(1)}, u32[]{:S(2)}) copy-start(f32[16,1024]{1,0:T(8,128)S(1)} %get-tuple-element.741) | copy-start | bytes 196612 | tf_op jit(solution)/shard_map/while
  1371.7 35.2 %copy-start.45 = (f32[16,1024]{1,0:T(8,128)}, f32[16,1024]{1,0:T(8,128)S(1)}, u32[]{:S(2)}) copy-start(f32[16,1024]{1,0:T(8,128)S(1)} %get-tuple-element.739) | copy-start | bytes 196612 | tf_op jit(solution)/shard_map/while
  1466.2 12.5 collective-permute-start.1
  (94 other events, 745.0 us)
Sparse Core Ops, SparseCore 0:
  9.6 19.4 all-gather.12
  48.4 11.8 all-gather.14
  415.6 18.2 all-gather.16
  487.3 17.9 reduce-scatter.7
  812.4 18.2 all-gather.18
  897.0 17.9 reduce-scatter.9
  971.8 180.1 reduce-scatter.15
  1154.9 147.8 reduce-scatter.13
  1497.0 173.9 reduce-scatter.11
where the time goes:
time: 1690 us; the launch traced here: 1680 us
  matrix products  609 us (36%)
  blocking collectives  293 us (17%)
  local copies, waits for them, and re-layouts  287 us (17%)
  waiting for transfers between devices  255 us (15%)
  other arithmetic  192 us (11%)
  starting transfers between devices  20.1 us (1%)
    unnamed x161, local copies, waits for them, and re-layouts  122 us
    all_to_all x1, blocking collectives, body(): lax.all_to_all(dispatch(d_expert_value), 'expert', split_axis=0, concat_a...  114 us
    all_to_all x1, blocking collectives, body(): lax.all_to_all(dispatch(mixed_low), 'expert', split_axis=0, concat_axis=1...  101 us
    dot_general x4, matrix products, backward_block(): jnp.einsum('qhd,khd->hqk', d_context_heads, value_heads, preferred_elemen...  82.9 us
    all_to_all x1, waiting for transfers between devices, body(): lax.all_to_all(d_rows, 'expert', split_axis=1, concat_axis=0, tiled=True)  78.2 us
    all_to_all x1, waiting for transfers between devices, body(): lax.all_to_all(expert_rows, 'expert', split_axis=1, concat_axis=0, tiled=...  77.5 us
    dot_general x4, matrix products, forward_block(): jnp.einsum('hqk,khd->hqd', weights.astype(jnp.bfloat16), value_heads, pre...  67.7 us
    dot_general x4, matrix products, backward_block(): jnp.einsum('hqk,qhd->khd', probs_part.astype(jnp.bfloat16), d_context_hea...  62 us
  transfers between devices with their start and end apart: 13, of which 8 were waited for; matrix products, arithmetic and copies ran while one was open for 46% of the time, Pallas kernels for 0%

commit v1 on v0

--- a/solution.py
+++ b/solution.py
@@ -4,10 +4,20 @@
 import jax.numpy as jnp
 from jax import lax
 from jax.sharding import PartitionSpec as P
+from jax.lax import all_to_all, axis_size
 
 HEAD_DIM = 64
 NORM_EPSILON = 1e-05
 MASK_FILL = -1e30
+
+
+def _plan_sectors(local, array_axis, in_dim):
+    oldest = axis_size("expert")
+    z = jnp.split(local, oldest, axis=array_axis)
+    local_next = jnp.stack(z)
+    state_now = all_to_all(local_next, axis_name="expert", split_axis=0, concat_axis=0)
+    next_value = jnp.concatenate(state_now, axis=in_dim)
+    return next_value
 
 
 def passed_along(array, axis, by):
@@ -196,9 +206,7 @@
     d_expert_bias = jnp.sum(out_cot, axis=0)
     d_gate = jnp.sum(out_cot * expert_value, axis=-1)
     d_expert_value = (gate_value[:, None] * out_cot).astype(jnp.bfloat16)
-    grads_arrived = lax.all_to_all(
-        dispatch(d_expert_value), "expert", split_axis=0, concat_axis=1, tiled=True
-    )
+    grads_arrived = _plan_sectors(dispatch(d_expert_value), 0, 1)
     unused_out, gelu_back = jax.vjp(partial(jax.nn.gelu, approximate=True), pre_act)
     grad_in = lax.all_gather(grads_arrived, "fsdp", axis=1, tiled=True)
     d_activ = jnp.einsum("erd,ehd->erh", grad_in, w_down, preferred_element_type=jnp.float32)

time: 1690 us -> 1700 us (level)
    unnamed x161 -> x176, local copies, waits for them, and re-layouts: 122 us -> 137 us
  transfers between devices with their start and end apart: 13 -> 13, of which waited for: 8 -> 8; matrix products, arithmetic and copies ran while one was open for 46% -> 45% of each run, Pallas kernels for 0% -> 0%
where the time goes in v1:
time: 1700 us; the launch traced here: 1690 us
  matrix products  609 us (36%)
  local copies, waits for them, and re-layouts  302 us (18%)
  blocking collectives  293 us (17%)
  waiting for transfers between devices  255 us (15%)
  other arithmetic  192 us (11%)
  starting transfers between devices  20.1 us (1%)
    unnamed x176, local copies, waits for them, and re-layouts  137 us
    all_to_all x1, blocking collectives, _plan_sectors(): all_to_all(local_next, axis_name='expert', split_axis=0, concat_axis=0)  113 us
    all_to_all x1, blocking collectives, body(): lax.all_to_all(dispatch(mixed_low), 'expert', split_axis=0, concat_axis=1...  101 us
    dot_general x4, matrix products, backward_block(): jnp.einsum('qhd,khd->hqk', d_context_heads, value_heads, preferred_elemen...  82.9 us
    all_to_all x1, waiting for transfers between devices, body(): lax.all_to_all(d_rows, 'expert', split_axis=1, concat_axis=0, tiled=True)  78.3 us
    all_to_all x1, waiting for transfers between devices, body(): lax.all_to_all(expert_rows, 'expert', split_axis=1, concat_axis=0, tiled=...  77.5 us
    dot_general x4, matrix products, forward_block(): jnp.einsum('hqk,khd->hqd', weights.astype(jnp.bfloat16), value_heads, pre...  67.7 us
    dot_general x4, matrix products, backward_block(): jnp.einsum('hqk,qhd->khd', probs_part.astype(jnp.bfloat16), d_context_hea...  62 us
  transfers between devices with their start and end apart: 13, of which 8 were waited for; matrix products, arithmetic and copies ran while one was open for 45% of the time, Pallas kernels for 0%

profile of v1, /device:TPU:0, one launch (start us, length us, event | category | flops | bytes accessed | tf_op | source)
XLA Modules:
  0.0 1693.2 jit_solution(4760277834244362283)
XLA Ops:
  91.9 196.8 %while.28 = (s32[]{:T(128)}, f32[16,1024]{1,0:T(8,128)S(1)}, f32[16,1024]{1,0:T(8,128)S(1)}, f32[16,1024,64]{1,2,0:T(8,128)}, s32[4]{0:T(128)S(1)}, /*index=5*/s...) while((s32[]{:T(128)}, f32[16,1024]{1,0:T(8,128)S(1)}, ...), condition=%wide.region_5.6_spmd.clone, body=%wide.region_2.5_spmd.clone.sunk | while | flops 2219395072 | bytes 120604920 | solution.py:165
  314.3 101.1 %all_to_all.41 = bf16[16,128,1024]{2,1,0:T(8,128)(2,1)} all-to-all(bf16[16,128,1024]{2,1,0:T(8,128)(2,1)} %bitcast.352), channel_id=1, replica_groups=mesh['fsdp'=2,'expert'=16] {'expert'}, dimensions={0} | all-to-all | bytes 8388608 | tf_op jit(solution)/shard_map/all_to_all | solution.py:194
  415.5 18.4 %all-gather.17.cloned.1.call-done = bf16[1,4096,1024]{2,1,0:T(8,128)(2,1)} async-done(((bf16[1,2048,1024]{2,1,0:T(8,128)(2,1)}), bf16[1,4096,1024]{2,1,0:T(8,128)(2,1)}) %all-gather.17.cloned.1.call-update) | async-done | bytes 8388624 | tf_op jit(solution)/shard_map/all_gather | solution.py:195
  433.9 25.7 %fusion.38 = f32[4096,2048]{1,0:T(8,128)} fusion(bf16[1,4096,1024]{2,1,0:T(8,128)(2,1)} %all-gather.17.cloned.1.call-done, bf16[1,1024,2048]{2,1,0:T(8,128)(2,1)} %param.36), kind=kOutput, calls=%fused_computation.63 | convolution fusion | flops 17179869184 | bytes 46137344 | tf_op jit(solution)/shard_map/erd,edh->erh/dot_general | solution.py:196
  459.6 27.6 %convert_bitcast_fusion.1 = bf16[1,4096,1024]{2,1,0:T(8,128)(2,1)} fusion(bf16[1,2048,1024]{2,1,0:T(8,128)(2,1)S(1)} %copy-done.73, f32[4096,2048]{1,0:T(8,128)} %fusion.38), kind=kOutput, calls=%fused_computation.66 | convolution fusion | flops 17259560960 | bytes 46137344 | tf_op jit(solution)/shard_map/erh,ehd->erd/dot_general | solution.py:198
  514.6 26.0 %reduce.9 = bf16[2048,1024]{1,0:T(8,128)(2,1)} reduce(bf16[2048,1,1024]{2,1,0:T(2,128)(2,1)} %bitcast.345, bf16[]{:T(256)} %broadcast.411), dimensions={1}, to_apply=%bitcast.275.reduce_sub_computation | reduce | bytes 8388610
  561.9 77.5 %all-to-all-done.1 = bf16[16,2,65536]{2,1,0:T(2,128)(2,1)} async-done(((bf16[16,2,65536]{2,1,0:T(2,128)(2,1)}), bf16[16,2,65536]{2,1,0:T(2,128)(2,1)}, u32[]{:S(2)}, u32[]{:S(2)}) %all-to-all-start.1) | async-done | bytes 4194336 | tf_op jit(solution)/shard_map/all_to_all | solution.py:202
  658.8 20.9 %gather_fusion = bf16[1024,1024]{1,0:T(8,128)(2,1)} fusion(bf16[16,128,1024]{2,1,0:T(8,128)(2,1)} %bitcast.342, s32[1024]{0:T(1024)S(1)} %bitcast.338), kind=kCustom, calls=%fused_computation | custom fusion | bytes 4202496 | tf_op jit(solution)/shard_map/gather | solution.py:192
  714.2 113.4 %all_to_all.42 = bf16[16,1,128,1024]{3,2,1,0:T(8,128)(2,1)} all-to-all(bf16[16,1,128,1024]{3,2,1,0:T(8,128)(2,1)S(1)} %fusion.88), channel_id=1, replica_groups=mesh['fsdp'=2,'expert'=16] {'expert'}, dimensions={0} | all-to-all | bytes 8388608 | tf_op jit(solution)/shard_map/all_to_all | solution.py:18
  827.7 18.4 %all-gather.19.cloned.1.call-done = bf16[1,4096,1024]{2,1,0:T(8,128)(2,1)} async-done(((bf16[1,2048,1024]{2,1,0:T(8,128)(2,1)}), bf16[1,4096,1024]{2,1,0:T(8,128)(2,1)}) %all-gather.19.cloned.1.call-update) | async-done | bytes 8388624 | tf_op jit(solution)/shard_map/all_gather | solution.py:211
  846.1 42.2 %fusion.31 = bf16[4096,2048]{1,0:T(8,128)(2,1)} fusion(f32[4096,2048]{1,0:T(8,128)} %fusion.38, bf16[1,4096,1024]{2,1,0:T(8,128)(2,1)} %all-gather.19.cloned.1.call-done, bf16[1,2048,1024]{2,1,0:T(8,128)(2,1)} %param.37), kind=kOutput, calls=%fused_computation.52 | convolution fusion | flops 17347641344 | bytes 62914560 | tf_op jit(solution)/shard_map/erd,ehd->erh/dot_general | solution.py:212
  888.3 23.9 %convert_bitcast_fusion = bf16[1,4096,1024]{2,1,0:T(8,128)(2,1)} fusion(bf16[4096,2048]{1,0:T(8,128)(2,1)} %fusion.31, bf16[1,1024,2048]{2,1,0:T(8,128)(2,1)} %param.36), kind=kOutput, calls=%fused_computation.65 | convolution fusion | flops 17184063488 | bytes 29360128 | tf_op jit(solution)/shard_map/erh,edh->erd/dot_general | solution.py:218
  912.2 18.1 %reduce-scatter.10.cloned.1.call-done = bf16[1,2048,1024]{2,1,0:T(8,128)(2,1)} async-done(((bf16[1,4096,1024]{2,1,0:T(8,128)(2,1)}), bf16[1,2048,1024]{2,1,0:T(8,128)(2,1)}) %reduce-scatter.10.cloned.1.call-update) | async-done | bytes 4194320 | tf_op jit(solution)/shard_map/reduce_scatter | solution.py:219
  939.0 26.0 %reduce.10 = bf16[2048,1024]{1,0:T(8,128)(2,1)} reduce(bf16[2048,1,1024]{2,1,0:T(2,128)(2,1)} %bitcast.346, bf16[]{:T(256)} %broadcast.411), dimensions={1}, to_apply=%bitcast.274.reduce_sub_computation | reduce | bytes 8388610
  987.1 78.3 %all-to-all-done.3 = bf16[16,2,65536]{2,1,0:T(2,128)(2,1)} async-done(((bf16[16,2,65536]{2,1,0:T(2,128)(2,1)}), bf16[16,2,65536]{2,1,0:T(2,128)(2,1)}, u32[]{:S(2)}, u32[]{:S(2)}) %all-to-all-start.3) | async-done | bytes 4194336 | tf_op jit(solution)/shard_map/all_to_all | solution.py:223
  1124.2 351.3 %while.29 = (s32[]{:T(128)}, f32[1024,16,64]{0,2,1:T(8,128)}, f32[4,512,2048]{2,1,0:T(8,128)}, s32[4]{0:T(128)S(1)}, bf16[2048,2048]{0,1:T(8,128)(2,1)}, /*index...) while((s32[]{:T(128)}, f32[1024,16,64]{0,2,1:T(8,128)}, ...), condition=%wide.region_23.24_spmd.clone, body=%wide.region_22.23_spmd.clone.sunk | while | flops 5440538624 | bytes 305875520 | solution.py:264
  1159.8 20.7 %fusion.199 = bf16[16,1024,512]{1,2,0:T(8,128)(2,1)} fusion(f32[16,512,1024]{2,1,0:T(8,128)} %fusion.198, f32[16,1024]{1,0:T(8,128)S(1)} %get-tuple-element.741, f32[16,1024]{1,0:T(8,128)S(1)} %get-tuple-element.739, pred[1024,512]{0,1:T(8,128)(4,1)S(1)} %copy-done.21, bf16[512,16,64]{0,2,1:T(8,128)(2,1)S(1)} %bitcast.349, ...), kind=kOutput, calls=%fused_computation.30.clone.1 | convolution fusion | flops 1115684864 | bytes 54132736 | tf_op jit(solution)/shard_map/while/body/eval_jaxpr/qhd,khd->hqk/dot_general | solution.py:246
  1245.9 20.8 %fusion.199 = bf16[16,1024,512]{1,2,0:T(8,128)(2,1)} fusion(f32[16,512,1024]{2,1,0:T(8,128)} %fusion.198, f32[16,1024]{1,0:T(8,128)S(1)} %get-tuple-element.741, f32[16,1024]{1,0:T(8,128)S(1)} %get-tuple-element.739, pred[1024,512]{0,1:T(8,128)(4,1)S(1)} %copy-done.21, bf16[512,16,64]{0,2,1:T(8,128)(2,1)S(1)} %bitcast.349, ...), kind=kOutput, calls=%fused_computation.30.clone.1 | convolution fusion | flops 1115684864 | bytes 54132736 | tf_op jit(solution)/shard_map/while/body/eval_jaxpr/qhd,khd->hqk/dot_general | solution.py:246
  1334.3 20.7 %fusion.199 = bf16[16,1024,512]{1,2,0:T(8,128)(2,1)} fusion(f32[16,512,1024]{2,1,0:T(8,128)} %fusion.198, f32[16,1024]{1,0:T(8,128)S(1)} %get-tuple-element.741, f32[16,1024]{1,0:T(8,128)S(1)} %get-tuple-element.739, pred[1024,512]{0,1:T(8,128)(4,1)S(1)} %copy-done.21, bf16[512,16,64]{0,2,1:T(8,128)(2,1)S(1)} %bitcast.349, ...), kind=kOutput, calls=%fused_computation.30.clone.1 | convolution fusion | flops 1115684864 | bytes 54132736 | tf_op jit(solution)/shard_map/while/body/eval_jaxpr/qhd,khd->hqk/dot_general | solution.py:246
  1422.4 20.7 %fusion.199 = bf16[16,1024,512]{1,2,0:T(8,128)(2,1)} fusion(f32[16,512,1024]{2,1,0:T(8,128)} %fusion.198, f32[16,1024]{1,0:T(8,128)S(1)} %get-tuple-element.741, f32[16,1024]{1,0:T(8,128)S(1)} %get-tuple-element.739, pred[1024,512]{0,1:T(8,128)(4,1)S(1)} %copy-done.21, bf16[512,16,64]{0,2,1:T(8,128)(2,1)S(1)} %bitcast.349, ...), kind=kOutput, calls=%fused_computation.30.clone.1 | convolution fusion | flops 1115684864 | bytes 54132736 | tf_op jit(solution)/shard_map/while/body/eval_jaxpr/qhd,khd->hqk/dot_general | solution.py:246
  1515.7 24.1 %fusion.51 = f32[1,1024,2048]{2,1,0:T(8,128)} fusion(bf16[4096,2048]{1,0:T(8,128)(2,1)} %fusion.31, bf16[1,4096,1024]{2,1,0:T(8,128)(2,1)} %all-gather.17.cloned.1.call-done), kind=kOutput, calls=%fused_computation.84 | convolution fusion | flops 17179869184 | bytes 33554432 | tf_op jit(solution)/shard_map/erd,erh->edh/dot_general | solution.py:217
  1539.8 26.9 %fusion.54 = f32[1,2048,1024]{2,1,0:T(8,128)} fusion(bf16[1,4096,1024]{2,1,0:T(8,128)(2,1)} %all-gather.19.cloned.1.call-done, f32[4096,2048]{1,0:T(8,128)} %fusion.38), kind=kOutput, calls=%fused_computation.85 | convolution fusion | flops 17255366656 | bytes 50331648 | tf_op jit(solution)/shard_map/erh,erd->ehd/dot_general | solution.py:213
  1594.2 59.0 %all-reduce.8 = (f32[1024]{0:T(1024)S(1)}, f32[1024]{0:T(1024)S(1)}, f32[1024]{0:T(1024)S(1)}, f32[1024]{0:T(1024)S(1)}, f32[1024]{0:T(1024)S(1)}, /*index=5*/f3...) all-reduce(f32[1024]{0:T(1024)S(1)} %get-tuple-element.402, ...), channel_id=4, replica_groups=mesh['fsdp'=2,'expert'=16] {'fsdp','expert'}, use_global_device_ids=true, to_apply=%region_27.28.clone | all-reduce | flops 8192 | bytes 65536
  1668.1 18.3 %reduce-scatter.12.cloned.1.call-done = f32[32,3072]{1,0:T(8,128)} async-done(((f32[1024,3072]{1,0:T(8,128)}), f32[32,3072]{1,0:T(8,128)}) %reduce-scatter.12.cloned.1.call-update) | async-done | bytes 393232 | tf_op jit(solution)/shard_map/reduce_scatter | solution.py:288
  (477 shorter events, 842.9 us)
Async XLA Ops:
  7.2 21.9 %all-gather.13.cloned.1.call-start = ((), (), s32[]{:S(2)}) async-start(), calls=%async_computation.9 | async-start | bytes 9437184 | tf_op jit(solution)/shard_map/all_gather | solution.py:84
  7.9 285.7 %all-gather.15.cloned.1.call-start = ((), (), s32[]{:S(2)}) async-start(), calls=%async_computation.10 | async-start | bytes 3145728 | tf_op jit(solution)/shard_map/all_gather | solution.py:87
  44.1 24.8 %collective-permute-start = (bf16[1024,2048]{1,0:T(8,128)(2,1)}, bf16[1024,2048]{1,0:T(8,128)(2,1)}, u32[]{:S(2)}, u32[]{:S(2)}) collective-permute-start(bf16[1024,2048]{1,0:T(8,128)(2,1)} %pad_maximum_fusion.1), channel_id=1, source_target_pairs={{0,16},{1,17},{2,18},{3,19},{4,20},{5,21},{6,22},{7,23},{8,24},{9,... | collective-permute-start | bytes 12582920 | tf_op jit(solution)/shard_map/ppermute | solution.py:26
  48.2 385.6 %all-gather.17.cloned.1.call-start = ((), (), s32[]{:S(2)}) async-start(), calls=%async_computation.11 | async-start | bytes 12582912 | tf_op jit(solution)/shard_map/all_gather | solution.py:195
  304.8 110.6 %copy-start.40 = (f32[1024]{0:T(1024)}, f32[1024]{0:T(1024)S(1)}, u32[]{:S(2)}) copy-start(f32[1024]{0:T(1024)S(1)} %get-tuple-element.487) | copy-start | bytes 12292
  304.9 110.6 %copy-start.57 = (f32[1024]{0:T(1024)}, f32[1024]{0:T(1024)S(1)}, u32[]{:S(2)}) copy-start(f32[1024]{0:T(1024)S(1)} %fusion.110) | copy-start | bytes 12292
  415.5 89.9 %reduce-scatter.8.cloned.1.call-start = ((), (), s32[]{:S(2)}) async-start(), calls=%async_computation.12 | async-start | bytes 12582912 | tf_op jit(solution)/shard_map/reduce_scatter | solution.py:199
  552.0 87.4 %all-to-all-start.1 = ((bf16[16,2,65536]{2,1,0:T(2,128)(2,1)}), bf16[16,2,65536]{2,1,0:T(2,128)(2,1)}, u32[]{:S(2)}, u32[]{:S(2)}) async-start(bf16[16,2,65536]{2,1,0:T(2,128)(2,1)} %reshape.491), calls=%async_computation.2 | async-start | bytes 8388608 | tf_op jit(solution)/shard_map/all_to_all | solution.py:202
  559.0 287.1 %all-gather.19.cloned.1.call-start = ((), (), s32[]{:S(2)}) async-start(), calls=%async_computation.13 | async-start | bytes 12582912 | tf_op jit(solution)/shard_map/all_gather | solution.py:211
  561.9 121.7 %copy-start.12 = (bf16[1,1024,1024]{1,2,0:T(8,128)(2,1)}, bf16[1,1024,1024]{1,2,0:T(8,128)(2,1)S(1)}, u32[]{:S(2)}) copy-start(bf16[1,1024,1024]{1,2,0:T(8,128)(2,1)S(1)} %copy.135) | copy-start | bytes 6291460
  827.7 102.7 %reduce-scatter.10.cloned.1.call-start = ((), (), s32[]{:S(2)}) async-start(), calls=%async_computation.14 | async-start | bytes 12582912 | tf_op jit(solution)/shard_map/reduce_scatter | solution.py:219
  976.4 88.9 %all-to-all-start.3 = ((bf16[16,2,65536]{2,1,0:T(2,128)(2,1)}), bf16[16,2,65536]{2,1,0:T(2,128)(2,1)}, u32[]{:S(2)}, u32[]{:S(2)}) async-start(bf16[16,2,65536]{2,1,0:T(2,128)(2,1)} %reshape.493), calls=%async_computation.5 | async-start | bytes 8388608 | tf_op jit(solution)/shard_map/all_to_all | solution.py:223
  983.5 530.8 %reduce-scatter.16.cloned.1.call-start = ((), (), s32[]{:S(2)}) async-start(), calls=%async_computation.17 | async-start | bytes 540672
  987.0 681.1 %reduce-scatter.14.cloned.1.call-start = ((), (), s32[]{:S(2)}) async-start(), calls=%async_computation.16 | async-start | bytes 4325376 | tf_op jit(solution)/shard_map/reduce_scatter | solution.py:293
  1122.7 563.7 %reduce-scatter.12.cloned.1.call-start = ((), (), s32[]{:S(2)}) async-start(), calls=%async_computation.15 | async-start | bytes 12976128 | tf_op jit(solution)/shard_map/reduce_scatter | solution.py:288
  1124.4 35.3 %copy-start.36 = (f32[16,1024]{1,0:T(8,128)}, f32[16,1024]{1,0:T(8,128)S(1)}, u32[]{:S(2)}) copy-start(f32[16,1024]{1,0:T(8,128)S(1)} %get-tuple-element.741) | copy-start | bytes 196612 | tf_op jit(solution)/shard_map/while
  1124.4 35.3 %copy-start.45 = (f32[16,1024]{1,0:T(8,128)}, f32[16,1024]{1,0:T(8,128)S(1)}, u32[]{:S(2)}) copy-start(f32[16,1024]{1,0:T(8,128)S(1)} %get-tuple-element.739) | copy-start | bytes 196612 | tf_op jit(solution)/shard_map/while
  1210.4 35.5 %copy-start.36 = (f32[16,1024]{1,0:T(8,128)}, f32[16,1024]{1,0:T(8,128)S(1)}, u32[]{:S(2)}) copy-start(f32[16,1024]{1,0:T(8,128)S(1)} %get-tuple-element.741) | copy-start | bytes 196612 | tf_op jit(solution)/shard_map/while
  1210.5 35.4 %copy-start.45 = (f32[16,1024]{1,0:T(8,128)}, f32[16,1024]{1,0:T(8,128)S(1)}, u32[]{:S(2)}) copy-start(f32[16,1024]{1,0:T(8,128)S(1)} %get-tuple-element.739) | copy-start | bytes 196612 | tf_op jit(solution)/shard_map/while
  1299.0 35.3 %copy-start.36 = (f32[16,1024]{1,0:T(8,128)}, f32[16,1024]{1,0:T(8,128)S(1)}, u32[]{:S(2)}) copy-start(f32[16,1024]{1,0:T(8,128)S(1)} %get-tuple-element.741) | copy-start | bytes 196612 | tf_op jit(solution)/shard_map/while
  1299.0 35.3 %copy-start.45 = (f32[16,1024]{1,0:T(8,128)}, f32[16,1024]{1,0:T(8,128)S(1)}, u32[]{:S(2)}) copy-start(f32[16,1024]{1,0:T(8,128)S(1)} %get-tuple-element.739) | copy-start | bytes 196612 | tf_op jit(solution)/shard_map/while
  1387.1 35.2 %copy-start.36 = (f32[16,1024]{1,0:T(8,128)}, f32[16,1024]{1,0:T(8,128)S(1)}, u32[]{:S(2)}) copy-start(f32[16,1024]{1,0:T(8,128)S(1)} %get-tuple-element.741) | copy-start | bytes 196612 | tf_op jit(solution)/shard_map/while
  1387.2 35.2 %copy-start.45 = (f32[16,1024]{1,0:T(8,128)}, f32[16,1024]{1,0:T(8,128)S(1)}, u32[]{:S(2)}) copy-start(f32[16,1024]{1,0:T(8,128)S(1)} %get-tuple-element.739) | copy-start | bytes 196612 | tf_op jit(solution)/shard_map/while
  1481.6 12.5 collective-permute-start.1
  (94 other events, 745.1 us)
Sparse Core Ops, SparseCore 0:
  9.6 19.4 all-gather.12
  48.4 11.8 all-gather.14
  415.6 18.2 all-gather.16
  487.3 17.9 reduce-scatter.7
  827.8 18.2 all-gather.18
  912.4 17.9 reduce-scatter.9
  987.1 179.9 reduce-scatter.15
  1170.1 146.1 reduce-scatter.13
  1512.5 173.9 reduce-scatter.11
